TPU v7x, 32 devices: a whole 2x2x4 slice. The times are simulated.
32 devices in a mesh: member: 2 (over core), tp: 16 (over z, y, x).
Axes of the slice: x: 2, y: 2, z: 4, core: 2. Of those that a mesh axis runs over, the one named last changes fastest.
Arguments:
- stream_in: bfloat16 [512, 4096], P(('member', 'tp')), may hold values from -6 to 6
- kv_cache: bfloat16 [512, 512, 2048], P(('member', 'tp')), may hold values from -400 to 400
- lengths: int32 [128], replicated, may hold values from 1 to 512
- targets: int32 [128], replicated, may hold values from 0 to 65535
- norm_gains: float32 [3, 4096], replicated, may hold values from 0.1 to 1.9
- w_qkv: bfloat16 [4096, 6144], P(None, 'tp'), may hold values from -0.09375 to 0.09375
- w_out: bfloat16 [4096, 4096], P('tp'), may hold values from -0.09375 to 0.09375
- w_gate_up: bfloat16 [2, 4096, 14336], P(None, None, 'tp'), may hold values from -0.09375 to 0.09375
- w_down: bfloat16 [14336, 4096], P('tp'), may hold values from -0.046875 to 0.046875
- lm_head: bfloat16 [4096, 65536], P(None, 'tp'), may hold values from -300 to 300
- fast_in: float32 [4, 2, 4096], P('member'), may hold values from 0.1 to 1.9
- fast_hidden: float32 [4, 3, 14336], P('member', None, 'tp'), may hold values from 0.1 to 1.9
- fast_out: float32 [4, 4096], P('member'), may hold values from 0.1 to 1.9
Outputs:
- mean_logits: bfloat16 [128, 65536], P(None, 'tp')
- token_logprob: float32 [128], replicated
Inputs may be any that keep to these rules, and one draw needn't show every extreme that they name: lengths is the same for all members.
All inputs are finite; a program needn't handle non-finite values.
Results may differ from a plain program's by a relative error of at most 0.02.
Values may be sent and summed in bfloat16 or wider, within the bound.
No kernel may reach another device: no remote copies, remote signals or barrier semaphores. Data moves between devices by JAX's collectives and lax.ppermute only.
A program may use at most 192 MiB of HBM per device.

v0:
```python
import jax
import jax.numpy as jnp
from jax import lax
from jax.sharding import PartitionSpec as P

HEADS = 32
KV = 8
HD = 128
CACHE = 512


ROPE_BASE = 500000.0


def rms_norm(values_in, gain):
    return (
        values_in
        * lax.rsqrt(jnp.mean(values_in * values_in, axis=-1, keepdims=True) + 1e-05)
        * gain
    )


def rotate(values_in, positions):
    half_dim = values_in.shape[-1] // 2
    frequency = ROPE_BASE ** (-jnp.arange(half_dim, dtype=jnp.float32) * 2.0 / values_in.shape[-1])
    angles = positions.astype(jnp.float32)[:, None, None] * frequency[None, None, :]
    lower_half = values_in[..., :half_dim]
    upper_half = values_in[..., half_dim:]
    return jnp.concatenate(
        [
            lower_half * jnp.cos(angles) - upper_half * jnp.sin(angles),
            upper_half * jnp.cos(angles) + lower_half * jnp.sin(angles),
        ],
        axis=-1,
    )


def attend(projected, cache_rows, positions):
    row_count = projected.shape[0]
    head_cols = HEADS * HD
    kv_cols = KV * HD
    queries = rotate(
        projected[:, :head_cols].astype(jnp.float32).reshape(row_count, HEADS, HD), positions
    ).astype(jnp.bfloat16)
    new_key = rotate(
        projected[:, head_cols : head_cols + kv_cols]
        .astype(jnp.float32)
        .reshape(row_count, KV, HD),
        positions,
    ).astype(jnp.bfloat16)
    new_value = projected[:, head_cols + kv_cols :].reshape(row_count, KV, HD)
    cache_keys = cache_rows[:, :, :kv_cols].reshape(row_count, CACHE, KV, HD)
    cache_values = cache_rows[:, :, kv_cols:].reshape(row_count, CACHE, KV, HD)
    grouped = queries.reshape(row_count, KV, HEADS // KV, HD)
    inv_root = HD ** (-0.5)
    cached = (
        jnp.einsum("rkgd,rckd->rkgc", grouped, cache_keys, preferred_element_type=jnp.float32)
        * inv_root
    )
    fresh = (
        jnp.einsum("rkgd,rkd->rkg", grouped, new_key, preferred_element_type=jnp.float32) * inv_root
    )
    in_cache = jnp.arange(CACHE)[None, :] < positions[:, None]
    cached = jnp.where(in_cache[:, None, None, :], cached, -1e30)
    peak = jnp.maximum(jnp.max(cached, axis=-1), fresh)
    weights = jnp.exp(cached - peak[..., None])
    fresh_w = jnp.exp(fresh - peak)
    total_sum = jnp.sum(weights, axis=-1) + fresh_w
    probs = (weights / total_sum[..., None]).astype(jnp.bfloat16)
    fresh_p = (fresh_w / total_sum).astype(jnp.bfloat16)
    result = jnp.einsum("rkgc,rckd->rkgd", probs, cache_values, preferred_element_type=jnp.float32)
    result = (
        result
        + fresh_p.astype(jnp.float32)[..., None] * new_value.astype(jnp.float32)[:, :, None, :]
    )
    return result.reshape(row_count, HEADS * HD).astype(jnp.bfloat16)


def body(
    stream_in,
    kv_cache,
    lengths,
    targets,
    norm_gains,
    w_qkv,
    w_out,
    w_gate_up,
    w_down,
    lm_head,
    fast_in,
    fast_hidden,
    fast_out,
):
    tp_count = lax.axis_size("tp")
    tp_rank = lax.axis_index("tp")
    mem_dev = fast_in.shape[0]
    batch_rows = lengths.shape[0]
    own_rows = stream_in.shape[0]
    all_rows = own_rows * tp_count
    width = stream_in.shape[1]
    first_row = tp_rank * own_rows
    positions = lax.dynamic_slice_in_dim(lengths, first_row % batch_rows, own_rows, 0)
    own_member = first_row // batch_rows
    own_scale = lax.dynamic_index_in_dim(fast_out, own_member, 0, keepdims=True)
    own_normed = rms_norm(stream_in.astype(jnp.float32), norm_gains[0]).astype(jnp.bfloat16)
    attn_in = lax.all_gather(own_normed, "tp", axis=0, tiled=True)
    projected = jnp.dot(attn_in, w_qkv, preferred_element_type=jnp.float32).astype(jnp.bfloat16)
    row_major = lax.all_to_all(projected, "tp", split_axis=0, concat_axis=1, tiled=True)
    attended = attend(row_major, kv_cache, positions)
    head_major = lax.all_to_all(attended, "tp", split_axis=1, concat_axis=0, tiled=True)
    picked = head_major
    attn_sum = lax.psum_scatter(
        jnp.dot(picked, w_out, preferred_element_type=jnp.float32),
        "tp",
        scatter_dimension=0,
        tiled=True,
    )
    middle = (stream_in.astype(jnp.float32) + attn_sum).astype(jnp.bfloat16)
    own_ffn = rms_norm(middle.astype(jnp.float32), norm_gains[1]).astype(jnp.bfloat16)
    ffn_in = lax.all_gather(own_ffn, "tp", axis=0, tiled=True)
    grouped = ffn_in.astype(jnp.float32).reshape(mem_dev, batch_rows, width)
    gate_in = (grouped * fast_in[:, 0][:, None, :]).astype(jnp.bfloat16).reshape(all_rows, width)
    up_in = (grouped * fast_in[:, 1][:, None, :]).astype(jnp.bfloat16).reshape(all_rows, width)
    hidden_cols = w_gate_up.shape[2]
    gate_act = (
        jnp.dot(gate_in, w_gate_up[0], preferred_element_type=jnp.float32).reshape(
            mem_dev, batch_rows, hidden_cols
        )
        * fast_hidden[:, 0][:, None, :]
    )
    up_act = (
        jnp.dot(up_in, w_gate_up[1], preferred_element_type=jnp.float32).reshape(
            mem_dev, batch_rows, hidden_cols
        )
        * fast_hidden[:, 1][:, None, :]
    )
    hidden = (
        (jax.nn.silu(gate_act) * up_act * fast_hidden[:, 2][:, None, :])
        .astype(jnp.bfloat16)
        .reshape(all_rows, hidden_cols)
    )
    picked = hidden
    down_sum = lax.psum_scatter(
        jnp.dot(picked, w_down, preferred_element_type=jnp.float32),
        "tp",
        scatter_dimension=0,
        tiled=True,
    )
    layer_out = (middle.astype(jnp.float32) + down_sum * own_scale).astype(jnp.bfloat16)
    own_final = rms_norm(layer_out.astype(jnp.float32), norm_gains[2]).astype(jnp.bfloat16)
    final_in = lax.all_gather(own_final, "tp", axis=0, tiled=True)
    logits = jnp.dot(final_in, lm_head, preferred_element_type=jnp.float32)
    vocab_cols = lm_head.shape[1]
    member_total = jnp.sum(logits.reshape(mem_dev, batch_rows, vocab_cols), axis=0)
    member_count = mem_dev * lax.axis_size("member")
    mean_logit = (
        lax.psum(member_total.astype(jnp.bfloat16), "member").astype(jnp.float32) / member_count
    )
    column_ids = tp_rank * vocab_cols + jnp.arange(vocab_cols)
    target_part = jnp.sum(
        jnp.where(column_ids[None, :] == targets[:, None], mean_logit, 0.0), axis=-1
    )
    local_peak = jnp.max(mean_logit, axis=-1)
    peak = lax.pmax(local_peak, "tp")
    exp_total, target_logit = lax.psum(
        (jnp.sum(jnp.exp(mean_logit - peak[:, None]), axis=-1), target_part), "tp"
    )
    token_logprob = target_logit - (peak + jnp.log(exp_total))
    return (mean_logit.astype(jnp.bfloat16), token_logprob)


def solution(mesh):
    in_specs = (
        P(("member", "tp"), None),
        P(("member", "tp"), None, None),
        P(),
        P(),
        P(),
        P(None, "tp"),
        P("tp", None),
        P(None, None, "tp"),
        P("tp", None),
        P(None, "tp"),
        P("member", None, None),
        P("member", None, "tp"),
        P("member", None),
    )
    out_specs = (P(None, "tp"), P())
    return jax.shard_map(body, mesh=mesh, in_specs=in_specs, out_specs=out_specs, check_vma=False)
```

profile of v0, /device:TPU:0, one launch (start us, length us, event | category | flops | bytes accessed | tf_op | source)
XLA Modules:
  0.0 622.7 jit_solution(10672102106241271460)
XLA Ops:
  7.2 1.7 fusion.49
  8.9 1.0 fusion.33
  10.0 1.7 fusion.35
  12.4 23.1 %fusion.48 = (bf16[16,512,1024]{2,1,0:T(8,128)(2,1)}, bf16[16,512,1024]{2,1,0:T(8,128)(2,1)}) fusion(bf16[16,512,2048]{2,1,0:T(8,128)(2,1)} %param.14), kind=kLoop, calls=%fused_computation.81 | loop fusion | bytes 67108864 | tf_op jit(solution)/shard_map/slice | solution.py:52
  35.5 39.4 %all-gather.4.cloned.1.call-done = bf16[256,4096]{1,0:T(8,128)(2,1)} async-done(((bf16[16,4096]{1,0:T(8,128)(2,1)}), bf16[256,4096]{1,0:T(8,128)(2,1)}) %all-gather.4.cloned.1.call-update) | async-done | bytes 2097168 | tf_op jit(solution)/shard_map/all_gather | solution.py:106
  74.9 3.5 convolution_convert_fusion
  78.5 4.4 all-to-all-start
  83.0 21.6 %copy.34 = bf16[16,512,1024]{1,2,0:T(8,128)(2,1)} copy(bf16[16,512,1024]{2,1,0:T(8,128)(2,1)} %get-tuple-element.13) | data formatting | bytes 33554432
  104.6 21.6 %copy.33 = bf16[16,512,1024]{1,2,0:T(8,128)(2,1)} copy(bf16[16,512,1024]{2,1,0:T(8,128)(2,1)} %get-tuple-element.12) | data formatting | bytes 33554432
  127.3 8.2 %fusion.51 = (f32[16,8,4]{2,1,0:T(8,128)S(1)}, f32[16,8,4,512]{3,2,1,0:T(4,128)S(1)}) fusion(bf16[16,512,8,128]{1,3,2,0:T(8,128)(2,1)} %bitcast.76, bf16[16,8,4,64]{3,2,1,0:T(4,128)(2,1)S(1)} %bitcast.92, bf16[16,8,4,64]{3,2,1,0:T(4,128)(2,1)S(1)} %bitcast.90, pred[16,512]{1,0:T(8,128)(4,1)S(1)} %iota_compare_fusion), kind=kOutput, calls=%fused_computation.84 | convolution fusion | flops 68156928 | bytes 17967104 | tf_op jit(solution)/shard_map/rkgd,rckd->rkgc/dot_general | solution.py:57
  136.3 8.4 %fusion.26 = bf16[16,8,4,128]{3,2,1,0:T(4,128)(2,1)S(1)} fusion(bf16[16,512,8,128]{1,3,2,0:T(8,128)(2,1)} %bitcast.77, f32[16,8,4,512]{3,2,1,0:T(4,128)S(1)} %get-tuple-element.36, f32[16,8,4]{2,1,0:T(8,128)S(1)} %get-tuple-element.20, f32[16,8,4]{2,1,0:T(8,128)S(1)} %multiply_maximum_fusion, f32[16,8,128]{2,1,0:T(8,128)S(1)} %bitcast.97, ...), kind=kOutput, calls=%fused_computation.24 | convolution fusion | flops 68091904 | bytes 18028544 | tf_op jit(solution)/shard_map/rkgc,rckd->rkgd/dot_general | solution.py:71
  144.8 14.5 %all_to_all.35 = bf16[16,16,256]{2,0,1:T(8,128)(2,1)S(1)} all-to-all(bf16[16,16,256]{2,0,1:T(8,128)(2,1)S(1)} %copy.26), channel_id=1, replica_groups=mesh['member'=2,'tp'=16] {'tp'}, dimensions={1} | all-to-all | bytes 262144 | tf_op jit(solution)/shard_map/all_to_all | solution.py:110
  159.3 2.7 fusion.52
  162.1 92.5 %reduce-scatter.3.cloned.1.call-done = f32[16,4096]{1,0:T(8,128)} async-done(((f32[256,4096]{1,0:T(8,128)}), f32[16,4096]{1,0:T(8,128)}) %reduce-scatter.3.cloned.1.call-update) | async-done | bytes 262160 | tf_op jit(solution)/shard_map/reduce_scatter | solution.py:112
  254.6 1.1 fusion.37
  255.7 0.8 fusion.39
  256.9 61.0 %all-gather.6.cloned.1.call-done = bf16[256,4096]{1,0:T(8,128)(2,1)} async-done(((bf16[16,4096]{1,0:T(8,128)(2,1)}), bf16[256,4096]{1,0:T(8,128)(2,1)}) %all-gather.6.cloned.1.call-update) | async-done | bytes 2097168 | tf_op jit(solution)/shard_map/all_gather | solution.py:120
  317.9 2.3 fusion.6
  320.2 5.6 fusion.11
  325.8 5.6 fusion.23
  331.5 4.4 fusion.53
  336.6 93.5 %reduce-scatter.5.cloned.1.call-done = f32[16,4096]{1,0:T(8,128)} async-done(((f32[256,4096]{1,0:T(8,128)}), f32[16,4096]{1,0:T(8,128)}) %reduce-scatter.5.cloned.1.call-update) | async-done | bytes 262160 | tf_op jit(solution)/shard_map/reduce_scatter | solution.py:143
  430.1 1.1 fusion.30
  431.2 0.8 fusion.32
  432.0 61.2 %all-gather.8.cloned.1.call-done = bf16[256,4096]{1,0:T(8,128)(2,1)} async-done(((bf16[16,4096]{1,0:T(8,128)(2,1)}), bf16[256,4096]{1,0:T(8,128)(2,1)}) %all-gather.8.cloned.1.call-update) | async-done | bytes 2097168 | tf_op jit(solution)/shard_map/all_gather | solution.py:151
  493.2 16.9 %fusion.54 = f32[256,4096]{1,0:T(8,128)} fusion(bf16[256,4096]{1,0:T(8,128)(2,1)} %all-gather.8.cloned.1.call-done, bf16[4096,4096]{1,0:T(8,128)(2,1)} %param.22), kind=kOutput, calls=%fused_computation.87 | convolution fusion | flops 8589934592 | bytes 39845888 | tf_op jit(solution)/shard_map/dot_general | solution.py:152
  510.1 3.9 reduce_sum.67
  514.1 18.4 %all-reduce.3.cloned.1.call-done = bf16[128,4096]{1,0:T(8,128)(2,1)} async-done(((bf16[128,4096]{1,0:T(8,128)(2,1)}), bf16[128,4096]{1,0:T(8,128)(2,1)}) %all-reduce.3.cloned.1.call-update) | async-done | bytes 1048592 | tf_op jit(solution)/shard_map/psum | solution.py:157
  532.5 1.5 fusion.8
  534.0 42.0 %pmax.7 = f32[128]{0:T(128)S(1)} all-reduce(f32[128]{0:T(128)S(1)} %fusion.8), channel_id=1, replica_groups=mesh['member'=2,'tp'=16] {'tp'}, use_global_device_ids=true, to_apply=%region_12.13 | all-reduce | flops 128 | bytes 1024 | tf_op jit(solution)/shard_map/pmax | solution.py:164
  576.0 2.9 exponential_reduce_fusion
  578.8 36.5 %all-reduce = (f32[128]{0:T(128)S(1)}, f32[128]{0:T(128)S(1)}) all-reduce(f32[128]{0:T(128)S(1)} %get-tuple-element.3, f32[128]{0:T(128)S(1)} %get-tuple-element.2), channel_id=1, replica_groups=mesh['member'=2,'tp'=16] {'tp'}, use_global_device_ids=true, to_apply=%region_10.11 | all-reduce | flops 256 | bytes 2048 | tf_op jit(solution)/shard_map/psum | solution.py:165
  (64 shorter events, 4.5 us)
Async XLA Ops:
  7.2 67.8 %copy-start = (bf16[4096,384]{1,0:T(8,128)(2,1)S(1)}, bf16[4096,384]{1,0:T(8,128)(2,1)}, u32[]{:S(2)}) copy-start(bf16[4096,384]{1,0:T(8,128)(2,1)} %param.18) | copy-start | bytes 9437188
  7.2 67.7 %all-gather.4.cloned.1.call-start = ((), (), s32[]{:S(2)}) async-start(), calls=%async_computation.4 | async-start | bytes 2228224 | tf_op jit(solution)/shard_map/all_gather | solution.py:106
  78.5 47.9 %all-to-all-start = ((bf16[16,16,384]{2,1,0:T(8,128)(2,1)}), bf16[16,16,384]{2,1,0:T(8,128)(2,1)S(1)}, u32[]{:S(2)}, u32[]{:S(2)}) async-start(bf16[16,16,384]{2,1,0:T(8,128)(2,1)} %bitcast.1), calls=%async_computation | async-start | bytes 393216 | tf_op jit(solution)/shard_map/all_to_all | solution.py:108
  82.9 171.7 %reduce-scatter.3.cloned.1.call-start = ((), (), s32[]{:S(2)}) async-start(), calls=%async_computation.5 | async-start | bytes 4456448 | tf_op jit(solution)/shard_map/reduce_scatter | solution.py:112
  136.2 23.1 %copy-start.2 = (bf16[256,4096]{1,0:T(8,128)(2,1)S(1)}, bf16[256,4096]{1,0:T(8,128)(2,1)}, u32[]{:S(2)}) copy-start(bf16[256,4096]{1,0:T(8,128)(2,1)} %param.19) | copy-start | bytes 6291460
  159.3 95.3 %copy-start.3 = (bf16[16,4096]{1,0:T(8,128)(2,1)S(1)}, bf16[16,4096]{1,0:T(8,128)(2,1)}, u32[]{:S(2)}) copy-start(bf16[16,4096]{1,0:T(8,128)(2,1)} %param.13) | copy-start | bytes 393220
  159.3 96.4 %copy-start.5 = (f32[1,4096]{1,0:T(1,128)S(1)}, f32[1,4096]{1,0:T(1,128)}, u32[]{:S(2)}) copy-start(f32[1,4096]{1,0:T(1,128)} %get-tuple-element.27) | copy-start | bytes 49156
  159.3 97.4 %copy-start.6 = (f32[2,3,896]{2,0,1:T(2,128)S(1)}, f32[2,3,896]{2,0,1:T(2,128)}, u32[]{:S(2)}) copy-start(f32[2,3,896]{2,0,1:T(2,128)} %param.24) | copy-start | bytes 64516
  162.0 94.8 %copy-start.4 = (f32[2,2,4096]{2,1,0:T(2,128)S(1)}, f32[2,2,4096]{2,1,0:T(2,128)}, u32[]{:S(2)}) copy-start(f32[2,2,4096]{2,1,0:T(2,128)} %param.23) | copy-start | bytes 196612
  162.0 155.9 %all-gather.6.cloned.1.call-start = ((), (), s32[]{:S(2)}) async-start(), calls=%async_computation.6 | async-start | bytes 2228224 | tf_op jit(solution)/shard_map/all_gather | solution.py:120
  256.5 173.6 %reduce-scatter.5.cloned.1.call-start = ((), (), s32[]{:S(2)}) async-start(), calls=%async_computation.7 | async-start | bytes 4456448 | tf_op jit(solution)/shard_map/reduce_scatter | solution.py:143
  320.1 11.3 %slice-start = ((s8[7340032]{0:T(1024)(128)(4,1)}), s8[4194304]{0:T(1024)(128)(4,1)S(1)}, s32[]{:S(2)}) async-start(s8[7340032]{0:T(1024)(128)(4,1)} %bitcast.78), calls=%async_computation.10 | async-start | bytes 8388608
  325.8 5.7 slice-start.1
  335.8 0.8 copy-start.7
  335.9 157.3 %all-gather.8.cloned.1.call-start = ((), (), s32[]{:S(2)}) async-start(), calls=%async_computation.8 | async-start | bytes 2228224 | tf_op jit(solution)/shard_map/all_gather | solution.py:151
  432.0 100.5 %all-reduce.3.cloned.1.call-start = ((), (), s32[]{:S(2)}) async-start(), calls=%async_computation.9 | async-start | bytes 2097152 | tf_op jit(solution)/shard_map/psum | solution.py:157
  510.1 65.8 %copy-start.8 = (s32[128]{0:T(128)S(1)}, s32[128]{0:T(128)}, u32[]{:S(2)}) copy-start(s32[128]{0:T(128)} %param.16) | copy-start | bytes 1540
  510.1 105.8 %copy-start.1 = (bf16[4096,384]{1,0:T(8,128)(2,1)S(1)}, bf16[4096,384]{1,0:T(8,128)(2,1)}, u32[]{:S(2)}) copy-start(bf16[4096,384]{1,0:T(8,128)(2,1)} %param.18) | copy-start | bytes 9437188
Sparse Core Ops, SparseCore 0:
  11.8 63.0 all-gather.3
  162.1 92.4 reduce-scatter.2
  257.9 59.8 all-gather.5
  336.0 94.0 reduce-scatter.4
  433.3 59.8 all-gather.7
  514.2 18.2 all-reduce.2
where the time goes:
time: 624 us; the launch traced here: 623 us
  waiting for transfers between devices  366 us (59%)
  blocking collectives  93 us (15%)
  local copies, waits for them, and re-layouts  69.1 us (11%)
  matrix products  55.7 us (9%)
  other arithmetic  19.6 us (3%)
  between operations  14.4 us (2%)
    reduce_scatter x1, waiting for transfers between devices, body(): lax.psum_scatter(jnp.dot(picked, w_down, preferred_element_type=jnp.float...  93.5 us
    reduce_scatter x1, waiting for transfers between devices, body(): lax.psum_scatter(jnp.dot(picked, w_out, preferred_element_type=jnp.float3...  92.5 us
    all_gather x1, waiting for transfers between devices, body(): final_in = lax.all_gather(own_final, 'tp', axis=0, tiled=True)  61.2 us
    all_gather x1, waiting for transfers between devices, body(): ffn_in = lax.all_gather(own_ffn, 'tp', axis=0, tiled=True)  61 us
    unnamed x28, local copies, waits for them, and re-layouts  44.1 us
    pmax x1, blocking collectives, body(): peak = lax.pmax(local_peak, 'tp')  42 us
    all_gather x1, waiting for transfers between devices, body(): attn_in = lax.all_gather(own_normed, 'tp', axis=0, tiled=True)  39.4 us
    psum x1, blocking collectives, body(): lax.psum((jnp.sum(jnp.exp(mean_logit - peak[:, None]), axis=-1), target_p...  36.5 us
  transfers between devices with their start and end apart: 7, of which 6 were waited for; matrix products, arithmetic and copies ran while one was open for 11% of the time, Pallas kernels for 0%

commit v1 on v0

v1 whole, which is shorter than its diff:
```python
import jax
import jax.numpy as jnp
from jax import lax
from jax.experimental import pallas as pl
from jax.experimental.pallas import tpu as pltpu
from jax.sharding import PartitionSpec as P

HEADS = 32
KV = 8
HD = 128


ROPE_BASE = 500000.0


def rms_norm(values_in, gain):
    return (
        values_in
        * lax.rsqrt(jnp.mean(values_in * values_in, axis=-1, keepdims=True) + 1e-05)
        * gain
    )


def swap_with(values, tp_count, mask):
    return lax.ppermute(values, "tp", [(i, i ^ mask) for i in range(tp_count)])


def far_digits(tp_count):
    digits, stride = [], 4
    while stride < tp_count:
        size = min(4, tp_count // stride)
        digits.append((stride, size))
        stride *= size
    return digits


def gather_far(block, tp_count):
    values = block[None]
    for stride, size in far_digits(tp_count):
        parts = [values] + [swap_with(values, tp_count, stride * j) for j in range(1, size)]
        values = jnp.concatenate(parts, axis=0)
    return values


def gather_near(values, tp_count):
    half = values.shape[-1] // 2
    left, right = values[..., :half], values[..., half:]
    left = jnp.stack([left, swap_with(left, tp_count, 2)], axis=1)
    right = jnp.stack([right, swap_with(right, tp_count, 1)], axis=1)
    left = jnp.stack([left, swap_with(left, tp_count, 1)], axis=2)
    right = jnp.stack([right, swap_with(right, tp_count, 2)], axis=2)
    right = jnp.swapaxes(right, 1, 2)
    return jnp.concatenate([left, right], axis=-1)


def gather_rows(block, tp_count):
    rows, width = block.shape
    return gather_near(gather_far(block, tp_count), tp_count).reshape(tp_count * rows, width)


def scatter_rows(partial, tp_count):
    wide, narrow = jnp.float32, jnp.bfloat16
    rows = partial.shape[0] // tp_count
    width = partial.shape[1]
    half = width // 2
    blocks = partial.reshape(tp_count // 4, 2, 2, rows, width)

    def add(kept, sent, mask):
        return kept + swap_with(sent.astype(narrow), tp_count, mask).astype(wide)

    left, right = blocks[..., :half], blocks[..., half:]
    left = add(left[:, :, 0], left[:, :, 1], 1)
    right = add(right[:, 0], right[:, 1], 2)
    left = add(left[:, 0], left[:, 1], 2)
    right = add(right[:, 0], right[:, 1], 1)
    total = jnp.concatenate([left, right], axis=-1)
    for stride, size in reversed(far_digits(tp_count)):
        total = total.reshape((size, -1) + total.shape[1:])
        kept = total[0]
        for j in range(1, size):
            kept = add(kept, total[j], stride * j)
        total = kept
    return total[0]


def reorder(blocks, rank):
    count = blocks.shape[0]
    step = 1
    while step < count:
        pairs = blocks.reshape((count // (2 * step), 2, step) + blocks.shape[1:])
        flipped = jnp.concatenate([pairs[:, 1:], pairs[:, :1]], axis=1)
        blocks = jnp.where((rank // step) % 2 == 1, flipped, pairs).reshape(blocks.shape)
        step *= 2
    return blocks


def attend_kernel(positions_ref, heads_ref, cos_ref, sin_ref, cache_ref, out_ref):
    kv_cols = KV * HD
    group = HEADS // KV
    position = positions_ref[pl.program_id(0)]
    heads = heads_ref[0].astype(jnp.float32)
    turned = heads[: HEADS + KV]
    turned = turned * cos_ref[0] + pltpu.roll(turned, HD // 2, 1) * sin_ref[0]
    queries = turned[:HEADS]
    new_key = turned[HEADS:].astype(jnp.bfloat16).astype(jnp.float32)
    new_value = heads[HEADS + KV :]
    flat_key = jnp.concatenate([new_key[i : i + 1] for i in range(KV)], axis=1)
    flat_value = jnp.concatenate([new_value[i : i + 1] for i in range(KV)], axis=1)
    own_block = (
        lax.broadcasted_iota(jnp.int32, (HEADS, kv_cols), 0) // group
        == lax.broadcasted_iota(jnp.int32, (HEADS, kv_cols), 1) // HD
    )
    spread = jnp.where(own_block, jnp.concatenate([queries] * KV, axis=1), 0.0).astype(jnp.bfloat16)
    inv_root = HD ** (-0.5)
    cached = (
        lax.dot_general(
            spread,
            cache_ref[0, :, :kv_cols],
            (((1,), (1,)), ((), ())),
            preferred_element_type=jnp.float32,
        )
        * inv_root
    )
    fresh = jnp.sum(spread.astype(jnp.float32) * flat_key, axis=1, keepdims=True) * inv_root
    in_cache = lax.broadcasted_iota(jnp.int32, cached.shape, 1) < position
    cached = jnp.where(in_cache, cached, -1e30)
    peak = jnp.maximum(jnp.max(cached, axis=1, keepdims=True), fresh)
    weights = jnp.exp(cached - peak)
    fresh_w = jnp.exp(fresh - peak)
    total_sum = jnp.sum(weights, axis=1, keepdims=True) + fresh_w
    probs = (weights / total_sum).astype(jnp.bfloat16)
    fresh_p = (fresh_w / total_sum).astype(jnp.bfloat16).astype(jnp.float32)
    result = lax.dot_general(
        probs,
        cache_ref[0, :, kv_cols:],
        (((1,), (0,)), ((), ())),
        preferred_element_type=jnp.float32,
    )
    result = jnp.where(own_block, result + fresh_p * flat_value, 0.0)
    folded = result[:, :HD]
    for i in range(1, KV):
        folded = folded + result[:, i * HD : (i + 1) * HD]
    out_ref[0] = folded.astype(jnp.bfloat16)


def rotation_tables(positions):
    half_dim = HD // 2
    frequency = ROPE_BASE ** (-jnp.arange(half_dim, dtype=jnp.float32) * 2.0 / HD)
    angles = positions.astype(jnp.float32)[:, None] * frequency[None, :]
    cos, sin = jnp.cos(angles), jnp.sin(angles)
    return (
        jnp.concatenate([cos, cos], axis=-1)[:, None, :],
        jnp.concatenate([-sin, sin], axis=-1)[:, None, :],
    )


def attend(projected, cache_rows, positions):
    row_count, cache_len, cache_cols = cache_rows.shape
    head_count = HEADS + 2 * KV
    cos, sin = rotation_tables(positions)
    heads = projected.reshape(row_count, head_count, HD)
    result = pl.pallas_call(
        attend_kernel,
        grid_spec=pltpu.PrefetchScalarGridSpec(
            num_scalar_prefetch=1,
            grid=(row_count,),
            in_specs=[
                pl.BlockSpec((1, head_count, HD), lambda r, pos: (r, 0, 0)),
                pl.BlockSpec((1, 1, HD), lambda r, pos: (r, 0, 0)),
                pl.BlockSpec((1, 1, HD), lambda r, pos: (r, 0, 0)),
                pl.BlockSpec((1, cache_len, cache_cols), lambda r, pos: (r, 0, 0)),
            ],
            out_specs=pl.BlockSpec((1, HEADS, HD), lambda r, pos: (r, 0, 0)),
        ),
        out_shape=jax.ShapeDtypeStruct((row_count, HEADS, HD), jnp.bfloat16),
    )(positions, heads, cos, sin, cache_rows)
    return result.reshape(row_count, HEADS * HD)


def body(
    stream_in,
    kv_cache,
    lengths,
    targets,
    norm_gains,
    w_qkv,
    w_out,
    w_gate_up,
    w_down,
    lm_head,
    fast_in,
    fast_hidden,
    fast_out,
):
    tp_count = lax.axis_size("tp")
    tp_rank = lax.axis_index("tp")
    mem_dev = fast_in.shape[0]
    batch_rows = lengths.shape[0]
    own_rows = stream_in.shape[0]
    all_rows = own_rows * tp_count
    width = stream_in.shape[1]
    first_row = tp_rank * own_rows
    positions = lax.dynamic_slice_in_dim(lengths, first_row % batch_rows, own_rows, 0)
    own_member = first_row // batch_rows
    own_scale = lax.dynamic_index_in_dim(fast_out, own_member, 0, keepdims=True)
    own_normed = rms_norm(stream_in.astype(jnp.float32), norm_gains[0]).astype(jnp.bfloat16)
    attn_in = gather_rows(own_normed, tp_count)
    projected = jnp.dot(attn_in, w_qkv, preferred_element_type=jnp.float32).astype(jnp.bfloat16)
    projected = reorder(projected.reshape(tp_count, own_rows, -1), tp_rank).reshape(projected.shape)
    row_major = lax.all_to_all(projected, "tp", split_axis=0, concat_axis=1, tiled=True)
    attended = attend(row_major, kv_cache, positions)
    head_major = lax.all_to_all(attended, "tp", split_axis=1, concat_axis=0, tiled=True)
    picked = reorder(head_major.reshape(tp_count, own_rows, -1), tp_rank).reshape(head_major.shape)
    attn_sum = scatter_rows(jnp.dot(picked, w_out, preferred_element_type=jnp.float32), tp_count)
    middle = (stream_in.astype(jnp.float32) + attn_sum).astype(jnp.bfloat16)
    own_ffn = rms_norm(middle.astype(jnp.float32), norm_gains[1]).astype(jnp.bfloat16)
    ffn_in = gather_rows(own_ffn, tp_count)
    fast_in = reorder(fast_in, own_member)
    fast_hidden = reorder(fast_hidden, own_member)
    grouped = ffn_in.astype(jnp.float32).reshape(mem_dev, batch_rows, width)
    gate_in = (grouped * fast_in[:, 0][:, None, :]).astype(jnp.bfloat16).reshape(all_rows, width)
    up_in = (grouped * fast_in[:, 1][:, None, :]).astype(jnp.bfloat16).reshape(all_rows, width)
    hidden_cols = w_gate_up.shape[2]
    gate_act = (
        jnp.dot(gate_in, w_gate_up[0], preferred_element_type=jnp.float32).reshape(
            mem_dev, batch_rows, hidden_cols
        )
        * fast_hidden[:, 0][:, None, :]
    )
    up_act = (
        jnp.dot(up_in, w_gate_up[1], preferred_element_type=jnp.float32).reshape(
            mem_dev, batch_rows, hidden_cols
        )
        * fast_hidden[:, 1][:, None, :]
    )
    hidden = (
        (jax.nn.silu(gate_act) * up_act * fast_hidden[:, 2][:, None, :])
        .astype(jnp.bfloat16)
        .reshape(all_rows, hidden_cols)
    )
    picked = hidden
    down_sum = scatter_rows(jnp.dot(picked, w_down, preferred_element_type=jnp.float32), tp_count)
    layer_out = (middle.astype(jnp.float32) + down_sum * own_scale).astype(jnp.bfloat16)
    own_final = rms_norm(layer_out.astype(jnp.float32), norm_gains[2]).astype(jnp.bfloat16)
    cores = lax.axis_size("member")
    core = lax.axis_index("member")
    piece = width // cores
    member_count = mem_dev * cores
    mine = jnp.zeros((own_rows, piece), jnp.float32)
    for step in range(cores):
        target = (core + step) % cores
        part = lax.dynamic_slice_in_dim(own_final, target * piece, piece, 1)
        if step:
            part = lax.ppermute(part, "member", [(i, (i + step) % cores) for i in range(cores)])
        mine = mine + part.astype(jnp.float32)
    far = gather_far(mine.astype(jnp.bfloat16), tp_count)
    far = far.reshape((mem_dev, -1) + far.shape[1:]).astype(jnp.float32)
    summed = jnp.sum(far, axis=0).astype(jnp.bfloat16)
    summed = gather_near(summed, tp_count).reshape(tp_count // mem_dev, own_rows, piece)
    summed = reorder(summed, tp_rank).reshape(batch_rows, piece)
    final_sum = jnp.zeros((batch_rows, width), jnp.bfloat16)
    for step in range(cores):
        part = summed
        if step:
            part = lax.ppermute(summed, "member", [(i, (i + step) % cores) for i in range(cores)])
        source = (core - step) % cores
        final_sum = lax.dynamic_update_slice_in_dim(final_sum, part, source * piece, 1)
    vocab_cols = lm_head.shape[1]
    mean_logit = jnp.dot(final_sum, lm_head, preferred_element_type=jnp.float32) / member_count
    column_ids = tp_rank * vocab_cols + jnp.arange(vocab_cols)
    target_part = jnp.sum(
        jnp.where(column_ids[None, :] == targets[:, None], mean_logit, 0.0), axis=-1
    )
    peak = jnp.max(mean_logit, axis=-1)
    exp_total = jnp.sum(jnp.exp(mean_logit - peak[:, None]), axis=-1)
    stats = jnp.stack([peak, exp_total, target_part])
    mask = 1
    while mask < tp_count:
        other = swap_with(stats, tp_count, mask)
        peak = jnp.maximum(stats[0], other[0])
        total = stats[1] * jnp.exp(stats[0] - peak) + other[1] * jnp.exp(other[0] - peak)
        stats = jnp.stack([peak, total, stats[2] + other[2]])
        mask *= 2
    peak, exp_total, target_logit = stats[0], stats[1], stats[2]
    token_logprob = target_logit - (peak + jnp.log(exp_total))
    return (mean_logit.astype(jnp.bfloat16), token_logprob)


def solution(mesh):
    in_specs = (
        P(("member", "tp"), None),
        P(("member", "tp"), None, None),
        P(),
        P(),
        P(),
        P(None, "tp"),
        P("tp", None),
        P(None, None, "tp"),
        P("tp", None),
        P(None, "tp"),
        P("member", None, None),
        P("member", None, "tp"),
        P("member", None),
    )
    out_specs = (P(None, "tp"), P())
    return jax.shard_map(body, mesh=mesh, in_specs=in_specs, out_specs=out_specs, check_vma=False)
```

time: 624 us -> 271 us (0.43)
  waiting for transfers between devices: 366 us -> 112 us
  blocking collectives: 93 us -> 10.8 us
  local copies, waits for them, and re-layouts: 69.1 us -> 15 us
  starting transfers between devices: 4.84 us -> 58.2 us
  matrix products: 55.7 us -> 25.9 us
  Pallas kernels: 0 us -> 22.9 us
  between operations: 14.4 us -> 1.6 us
    reduce_scatter x2 -> x0, waiting for transfers between devices: 186 us -> none  [the longest x1 93.5 us: body(): lax.psum_scatter(jnp.dot(picked, w_down, preferred_element_type=jnp.float...]
    all_gather x3 -> x0, waiting for transfers between devices: 162 us -> none  [the longest x1 61.2 us: body(): final_in = lax.all_gather(own_final, 'tp', axis=0, tiled=True)]
    ppermute x0 -> x41, waiting for transfers between devices: none -> 104 us  [the longest x39 101 us: swap_with(): return lax.ppermute(values, 'tp', [(i, i ^ mask) for i in range(tp_count)])]
    ppermute x0 -> x41, starting transfers between devices: none -> 50.7 us  [the longest x39 50.6 us: swap_with(): return lax.ppermute(values, 'tp', [(i, i ^ mask) for i in range(tp_count)])]
    pmax x1 -> x0, blocking collectives: 42 us -> none  [body(): peak = lax.pmax(local_peak, 'tp')]
    unnamed x28 -> x39, local copies, waits for them, and re-layouts: 44.1 us -> 5.77 us
    psum x1 -> x0, blocking collectives: 36.5 us -> none  [body(): lax.psum((jnp.sum(jnp.exp(mean_logit - peak[:, None]), axis=-1), target_p...]
    pallas_call x0 -> x1, Pallas kernels: none -> 22.9 us  [attend(): pl.pallas_call(attend_kernel, grid_spec=pltpu.PrefetchScalarGridSpec(num_...]
  transfers between devices with their start and end apart: 7 -> 42, of which waited for: 6 -> 32; matrix products, arithmetic and copies ran while one was open for 11% -> 6% of each run, Pallas kernels for 0% -> 0%
where the time goes in v1:
time: 271 us
  waiting for transfers between devices  112 us (41%)
  starting transfers between devices  58.2 us (21%)
  matrix products  25.9 us (10%)
  other arithmetic  24.6 us (9%)
  Pallas kernels  22.9 us (8%)
  local copies, waits for them, and re-layouts  15 us (6%)
  blocking collectives  10.8 us (4%)
    ppermute x39, waiting for transfers between devices, swap_with(): return lax.ppermute(values, 'tp', [(i, i ^ mask) for i in range(tp_count)])  101 us
    ppermute x39, starting transfers between devices, swap_with(): return lax.ppermute(values, 'tp', [(i, i ^ mask) for i in range(tp_count)])  50.6 us
    pallas_call x1, Pallas kernels, attend(): pl.pallas_call(attend_kernel, grid_spec=pltpu.PrefetchScalarGridSpec(num_...  22.9 us
    dot_general x1, matrix products, body(): jnp.dot(final_sum, lm_head, preferred_element_type=jnp.float32)  13.4 us
    all_to_all x1, blocking collectives, body(): lax.all_to_all(attended, 'tp', split_axis=1, concat_axis=0, tiled=True)  10.8 us
    all_to_all x1, starting transfers between devices, body(): lax.all_to_all(projected, 'tp', split_axis=0, concat_axis=1, tiled=True)  7.51 us
    all_to_all x1, waiting for transfers between devices, body(): lax.all_to_all(projected, 'tp', split_axis=0, concat_axis=1, tiled=True)  7.27 us
    unnamed x39, local copies, waits for them, and re-layouts  5.77 us
  transfers between devices with their start and end apart: 42, of which 32 were waited for; matrix products, arithmetic and copies ran while one was open for 6% of the time, Pallas kernels for 0%

profile of v1, /device:TPU:0, one launch (start us, length us, event | category | flops | bytes accessed | tf_op | source)
XLA Modules:
  0.0 270.5 jit_solution(13067902136134988896)
XLA Ops:
  3.8 3.1 %collective-permute-start = (bf16[1,16,4096]{2,1,0:T(8,128)(2,1)S(1)}, bf16[1,16,4096]{2,1,0:T(8,128)(2,1)S(1)}, u32[]{:S(2)}, u32[]{:S(2)}) collective-permute-start(bf16[1,16,4096]{2,1,0:T(8,128)(2,1)S(1)} %fusion.70), channel_id=1, source_target_pairs={{0,4},{1,5},{2,6},{3,7},{4,0},{5,1},{6,2},{7,3},{8,12},{9,13},{10,... | collective-permute-start | bytes 393224 | tf_op jit(solution)/shard_map/ppermute | solution.py:25
  7.0 2.6 collective-permute-start.1
  9.6 2.5 collective-permute-done
  12.0 7.8 %collective-permute-done.1 = bf16[1,16,4096]{2,1,0:T(8,128)(2,1)S(1)} collective-permute-done((bf16[1,16,4096]{2,1,0:T(8,128)(2,1)S(1)}, bf16[1,16,4096]{2,1,0:T(8,128)(2,1)S(1)}, u32[]{:S(2)}, u32[]{:S(2)}) %collective-permute-start.1) | collective-permute-done | bytes 131104 | tf_op jit(solution)/shard_map/ppermute | solution.py:25
  23.1 3.4 %collective-permute-done.5 = bf16[4,16,2048]{2,1,0:T(8,128)(2,1)S(1)} collective-permute-done((bf16[4,16,2048]{2,1,0:T(8,128)(2,1)S(1)}, bf16[4,16,2048]{2,1,0:T(8,128)(2,1)S(1)}, u32[]{:S(2)}, u32[]{:S(2)}) %collective-permute-start.5) | collective-permute-done | bytes 262176 | tf_op jit(solution)/shard_map/ppermute | solution.py:25
  32.2 7.2 %collective-permute-done.6 = bf16[4,2,16,2048]{3,2,0,1:T(8,128)(2,1)} collective-permute-done((bf16[4,2,16,2048]{3,2,0,1:T(8,128)(2,1)}, bf16[4,2,16,2048]{3,2,0,1:T(8,128)(2,1)}, u32[]{:S(2)}, u32[]{:S(2)}) %collective-permute-start.6) | collective-permute-done | bytes 524320 | tf_op jit(solution)/shard_map/ppermute | solution.py:25
  44.8 7.5 %all-to-all-start = ((bf16[16,16,384]{2,1,0:T(8,128)(2,1)}), bf16[16,16,384]{2,1,0:T(8,128)(2,1)S(1)}, u32[]{:S(2)}, u32[]{:S(2)}) async-start(bf16[16,16,384]{2,1,0:T(8,128)(2,1)} %bitcast.28), calls=%async_computation | async-start | bytes 393216 | tf_op jit(solution)/shard_map/all_to_all | solution.py:210
  53.1 7.3 %all-to-all-done = bf16[16,16,384]{2,1,0:T(8,128)(2,1)S(1)} async-done(((bf16[16,16,384]{2,1,0:T(8,128)(2,1)}), bf16[16,16,384]{2,1,0:T(8,128)(2,1)S(1)}, u32[]{:S(2)}, u32[]{:S(2)}) %all-to-all-start) | async-done | bytes 196640 | tf_op jit(solution)/shard_map/all_to_all | solution.py:210
  61.2 22.9 %shard_map.140 = bf16[16,32,128]{2,1,0:T(8,128)(2,1)} custom-call(s32[16]{0:T(128)} %get-tuple-element.13.positions_ref, bf16[16,48,128]{2,1,0:T(8,128)(2,1)} %reshape.436.heads_ref, f32[16,1,128]{2,1,0:T(1,128)} %bitcast.447, f32[16,1,128]{2,1,0:T(1,128)} %bitcast.448, bf16[16,512,2048]{2,1,0:T(8,128)(2,1)} %cache_ref.1), custom_call_target="tpu_custom_call" | custom-call | tf_op jit(solution)/shard_map/pallas_call | solution.py:162
  85.2 10.8 %all_to_all.32 = bf16[16,16,256]{2,0,1:T(8,128)(2,1)S(1)} all-to-all(bf16[16,16,256]{2,0,1:T(8,128)(2,1)S(1)} %copy.65), channel_id=1, replica_groups=mesh['member'=2,'tp'=16] {'tp'}, dimensions={1} | all-to-all | bytes 262144 | tf_op jit(solution)/shard_map/all_to_all | solution.py:212
  101.9 6.7 %collective-permute-done.7 = bf16[4,2,16,2048]{3,2,0,1:T(8,128)(2,1)S(1)} collective-permute-done((bf16[4,2,16,2048]{3,2,0,1:T(8,128)(2,1)S(1)}, bf16[4,2,16,2048]{3,2,0,1:T(8,128)(2,1)S(1)}, u32[]{:S(2)}, u32[]{:S(2)}) %collective-permute-start.7) | collective-permute-done | bytes 524320 | tf_op jit(solution)/shard_map/ppermute | solution.py:25
  110.8 2.8 %collective-permute-done.9 = bf16[4,2,16,2048]{3,2,0,1:T(8,128)(2,1)S(1)} collective-permute-done((bf16[4,2,16,2048]{3,2,0,1:T(8,128)(2,1)S(1)}, bf16[4,2,16,2048]{3,2,0,1:T(8,128)(2,1)S(1)}, u32[]{:S(2)}, u32[]{:S(2)}) %collective-permute-start.9) | collective-permute-done | bytes 524320 | tf_op jit(solution)/shard_map/ppermute | solution.py:25
  116.6 4.9 %collective-permute-done.10 = bf16[4,16,2048]{2,1,0:T(8,128)(2,1)S(1)} collective-permute-done((bf16[4,16,2048]{2,1,0:T(8,128)(2,1)S(1)}, bf16[4,16,2048]{2,1,0:T(8,128)(2,1)S(1)}, u32[]{:S(2)}, u32[]{:S(2)}) %collective-permute-start.10) | collective-permute-done | bytes 262176 | tf_op jit(solution)/shard_map/ppermute | solution.py:25
  123.0 3.1 %collective-permute-start.13 = (bf16[1,16,4096]{2,1,0:T(8,128)(2,1)S(1)}, bf16[1,16,4096]{2,1,0:T(8,128)(2,1)S(1)}, u32[]{:S(2)}, u32[]{:S(2)}) collective-permute-start(bf16[1,16,4096]{2,1,0:T(8,128)(2,1)S(1)} %get-tuple-element.37), channel_id=1, source_target_pairs={{0,12},{1,13},{2,14},{3,15},{4,8},{5,9},{6,10},{7,11},{8,4},{9,5},... | collective-permute-start | bytes 393224 | tf_op jit(solution)/shard_map/ppermute | solution.py:25
  126.2 2.4 collective-permute-done.11
  128.5 6.3 %collective-permute-done.12 = bf16[1,16,4096]{2,1,0:T(8,128)(2,1)S(1)} collective-permute-done((bf16[1,16,4096]{2,1,0:T(8,128)(2,1)S(1)}, bf16[1,16,4096]{2,1,0:T(8,128)(2,1)S(1)}, u32[]{:S(2)}, u32[]{:S(2)}) %collective-permute-start.12) | collective-permute-done | bytes 131104 | tf_op jit(solution)/shard_map/ppermute | solution.py:25
  135.2 2.5 collective-permute-start.14
  140.6 5.7 %collective-permute-done.15 = bf16[1,16,4096]{2,1,0:T(8,128)(2,1)S(1)} collective-permute-done((bf16[1,16,4096]{2,1,0:T(8,128)(2,1)S(1)}, bf16[1,16,4096]{2,1,0:T(8,128)(2,1)S(1)}, u32[]{:S(2)}, u32[]{:S(2)}) %collective-permute-start.15) | collective-permute-done | bytes 131104 | tf_op jit(solution)/shard_map/ppermute | solution.py:25
  148.1 4.9 %collective-permute-done.19 = bf16[4,16,2048]{2,1,0:T(8,128)(2,1)S(1)} collective-permute-done((bf16[4,16,2048]{2,1,0:T(8,128)(2,1)S(1)}, bf16[4,16,2048]{2,1,0:T(8,128)(2,1)S(1)}, u32[]{:S(2)}, u32[]{:S(2)}) %collective-permute-start.19) | collective-permute-done | bytes 262176 | tf_op jit(solution)/shard_map/ppermute | solution.py:25
  156.2 6.1 %collective-permute-done.20 = bf16[4,2,16,2048]{3,2,0,1:T(8,128)(2,1)S(1)} collective-permute-done((bf16[4,2,16,2048]{3,2,0,1:T(8,128)(2,1)S(1)}, bf16[4,2,16,2048]{3,2,0,1:T(8,128)(2,1)S(1)}, u32[]{:S(2)}, u32[]{:S(2)}) %collective-permute-start.20) | collective-permute-done | bytes 524320 | tf_op jit(solution)/shard_map/ppermute | solution.py:25
  167.6 5.6 %fusion.12 = f32[2,128,896]{2,1,0:T(8,128)S(1)} fusion(bf16[2,128,4096]{2,1,0:T(8,128)(2,1)S(1)} %bitcast.409, bf16[2,4096,896]{2,1,0:T(8,128)(2,1)} %param.20, f32[2,896]{1,0:T(2,128)S(1)} %get-tuple-element.86), kind=kOutput, calls=%fused_computation.19 | convolution fusion | flops 1879277568 | bytes 10361856 | tf_op jit(solution)/shard_map/dot_general | solution.py:225
  173.3 2.4 fusion.24
  175.8 2.4 fusion
  183.3 6.3 %collective-permute-done.21 = bf16[4,2,16,2048]{3,2,0,1:T(8,128)(2,1)S(1)} collective-permute-done((bf16[4,2,16,2048]{3,2,0,1:T(8,128)(2,1)S(1)}, bf16[4,2,16,2048]{3,2,0,1:T(8,128)(2,1)S(1)}, u32[]{:S(2)}, u32[]{:S(2)}) %collective-permute-start.21) | collective-permute-done | bytes 524320 | tf_op jit(solution)/shard_map/ppermute | solution.py:25
  194.4 3.0 %collective-permute-done.22 = bf16[4,16,2048]{2,1,0:T(8,128)(2,1)S(1)} collective-permute-done((bf16[4,16,2048]{2,1,0:T(8,128)(2,1)S(1)}, bf16[4,16,2048]{2,1,0:T(8,128)(2,1)S(1)}, u32[]{:S(2)}, u32[]{:S(2)}) %collective-permute-start.22) | collective-permute-done | bytes 262176 | tf_op jit(solution)/shard_map/ppermute | solution.py:25
  205.0 5.7 %collective-permute-done.26 = bf16[1,16,4096]{2,1,0:T(8,128)(2,1)S(1)} collective-permute-done((bf16[1,16,4096]{2,1,0:T(8,128)(2,1)S(1)}, bf16[1,16,4096]{2,1,0:T(8,128)(2,1)S(1)}, u32[]{:S(2)}, u32[]{:S(2)}) %collective-permute-start.26) | collective-permute-done | bytes 131104 | tf_op jit(solution)/shard_map/ppermute | solution.py:25
  217.1 5.6 %collective-permute-done.30 = bf16[1,16,2048]{2,1,0:T(8,128)(2,1)S(1)} collective-permute-done((bf16[1,16,2048]{2,1,0:T(8,128)(2,1)S(1)}, bf16[1,16,2048]{2,1,0:T(8,128)(2,1)S(1)}, u32[]{:S(2)}, u32[]{:S(2)}) %collective-permute-start.30) | collective-permute-done | bytes 65568 | tf_op jit(solution)/shard_map/ppermute | solution.py:25
  229.8 2.4 collective-permute-done.35
  239.3 13.4 %fusion.126 = (f32[128]{0:T(128)S(1)}, f32[128,4096]{1,0:T(8,128)S(1)}) fusion(bf16[128,4096]{1,0:T(8,128)(2,1)} %constant_dynamic-update-slice_fusion, bf16[4096,4096]{1,0:T(8,128)(2,1)} %param.22), kind=kOutput, calls=%fused_computation.250 | convolution fusion | flops 4296015872 | bytes 36700672 | tf_op jit(solution)/shard_map/dot_general | solution.py:269
  259.4 2.4 collective-permute-done.38
  263.1 2.4 collective-permute-done.39
  267.0 3.0 %collective-permute-done.40 = f32[3,128]{1,0:T(4,128)S(1)} collective-permute-done((f32[3,128]{1,0:T(4,128)S(1)}, f32[3,128]{1,0:T(4,128)S(1)}, u32[]{:S(2)}, u32[]{:S(2)}) %collective-permute-start.40) | collective-permute-done | bytes 1568 | tf_op jit(solution)/shard_map/ppermute | solution.py:25
  (216 shorter events, 94.0 us)
Async XLA Ops:
  3.8 8.2 %collective-permute-start = (bf16[1,16,4096]{2,1,0:T(8,128)(2,1)S(1)}, bf16[1,16,4096]{2,1,0:T(8,128)(2,1)S(1)}, u32[]{:S(2)}, u32[]{:S(2)}) collective-permute-start(bf16[1,16,4096]{2,1,0:T(8,128)(2,1)S(1)} %fusion.70), channel_id=1, source_target_pairs={{0,4},{1,5},{2,6},{3,7},{4,0},{5,1},{6,2},{7,3},{8,12},{9,13},{10,... | collective-permute-start | bytes 393224 | tf_op jit(solution)/shard_map/ppermute | solution.py:25
  7.0 12.9 %collective-permute-start.1 = (bf16[1,16,4096]{2,1,0:T(8,128)(2,1)S(1)}, bf16[1,16,4096]{2,1,0:T(8,128)(2,1)S(1)}, u32[]{:S(2)}, u32[]{:S(2)}) collective-permute-start(bf16[1,16,4096]{2,1,0:T(8,128)(2,1)S(1)} %fusion.70), channel_id=1, source_target_pairs={{0,8},{1,9},{2,10},{3,11},{4,12},{5,13},{6,14},{7,15},{8,0},{9,1},... | collective-permute-start | bytes 393224 | tf_op jit(solution)/shard_map/ppermute | solution.py:25
  9.5 10.3 %collective-permute-start.2 = (bf16[1,16,4096]{2,1,0:T(8,128)(2,1)S(1)}, bf16[1,16,4096]{2,1,0:T(8,128)(2,1)S(1)}, u32[]{:S(2)}, u32[]{:S(2)}) collective-permute-start(bf16[1,16,4096]{2,1,0:T(8,128)(2,1)S(1)} %fusion.70), channel_id=1, source_target_pairs={{0,12},{1,13},{2,14},{3,15},{4,8},{5,9},{6,10},{7,11},{8,4},{9,5},... | collective-permute-start | bytes 393224 | tf_op jit(solution)/shard_map/ppermute | solution.py:25
  20.0 6.4 %collective-permute-start.5 = (bf16[4,16,2048]{2,1,0:T(8,128)(2,1)S(1)}, bf16[4,16,2048]{2,1,0:T(8,128)(2,1)S(1)}, u32[]{:S(2)}, u32[]{:S(2)}) collective-permute-start(bf16[4,16,2048]{2,1,0:T(8,128)(2,1)S(1)} %get-tuple-element.43), channel_id=1, source_target_pairs={{0,1},{1,0},{2,3},{3,2},{4,5},{5,4},{6,7},{7,6},{8,9},{9,8},{10,11... | collective-permute-start | bytes 786440 | tf_op jit(solution)/shard_map/ppermute | solution.py:25
  21.6 7.7 %collective-permute-start.3 = (bf16[4,16,2048]{2,1,0:T(8,128)(2,1)S(1)}, bf16[4,16,2048]{2,1,0:T(8,128)(2,1)S(1)}, u32[]{:S(2)}, u32[]{:S(2)}) collective-permute-start(bf16[4,16,2048]{2,1,0:T(8,128)(2,1)S(1)} %get-tuple-element.44), channel_id=1, source_target_pairs={{0,2},{1,3},{2,0},{3,1},{4,6},{5,7},{6,4},{7,5},{8,10},{9,11},{10,... | collective-permute-start | bytes 786440 | tf_op jit(solution)/shard_map/ppermute | solution.py:25
  27.5 11.8 %collective-permute-start.6 = (bf16[4,2,16,2048]{3,2,0,1:T(8,128)(2,1)}, bf16[4,2,16,2048]{3,2,0,1:T(8,128)(2,1)}, u32[]{:S(2)}, u32[]{:S(2)}) collective-permute-start(bf16[4,2,16,2048]{3,2,0,1:T(8,128)(2,1)} %get-tuple-element.46), channel_id=1, source_target_pairs={{0,2},{1,3},{2,0},{3,1},{4,6},{5,7},{6,4},{7,5},{8,10},{9,11},{10,... | collective-permute-start | bytes 1572872 | tf_op jit(solution)/shard_map/ppermute | solution.py:25
  30.4 10.2 %collective-permute-start.4 = (bf16[4,2,16,2048]{3,2,0,1:T(8,128)(2,1)}, bf16[4,2,16,2048]{3,2,0,1:T(8,128)(2,1)}, u32[]{:S(2)}, u32[]{:S(2)}) collective-permute-start(bf16[4,2,16,2048]{3,2,0,1:T(8,128)(2,1)} %get-tuple-element.40), channel_id=1, source_target_pairs={{0,1},{1,0},{2,3},{3,2},{4,5},{5,4},{6,7},{7,6},{8,9},{9,8},{10,11... | collective-permute-start | bytes 1572872 | tf_op jit(solution)/shard_map/ppermute | solution.py:25
  44.8 15.6 %all-to-all-start = ((bf16[16,16,384]{2,1,0:T(8,128)(2,1)}), bf16[16,16,384]{2,1,0:T(8,128)(2,1)S(1)}, u32[]{:S(2)}, u32[]{:S(2)}) async-start(bf16[16,16,384]{2,1,0:T(8,128)(2,1)} %bitcast.28), calls=%async_computation | async-start | bytes 393216 | tf_op jit(solution)/shard_map/all_to_all | solution.py:210
  99.1 9.5 %collective-permute-start.7 = (bf16[4,2,16,2048]{3,2,0,1:T(8,128)(2,1)S(1)}, bf16[4,2,16,2048]{3,2,0,1:T(8,128)(2,1)S(1)}, u32[]{:S(2)}, u32[]{:S(2)}) collective-permute-start(bf16[4,2,16,2048]{3,2,0,1:T(8,128)(2,1)S(1)} %slice_bitcast_fusion.10), channel_id=1, source_target_pairs={{0,1},{1,0},{2,3},{3,2},{4,5},{5,4},{6,7},{7,6},{8,9},{9,8},{10,11... | collective-permute-start | bytes 1572872 | tf_op jit(solution)/shard_map/ppermute | solution.py:25
  101.6 12.1 %collective-permute-start.9 = (bf16[4,2,16,2048]{3,2,0,1:T(8,128)(2,1)S(1)}, bf16[4,2,16,2048]{3,2,0,1:T(8,128)(2,1)S(1)}, u32[]{:S(2)}, u32[]{:S(2)}) collective-permute-start(bf16[4,2,16,2048]{3,2,0,1:T(8,128)(2,1)S(1)} %slice_bitcast_fusion.8), channel_id=1, source_target_pairs={{0,2},{1,3},{2,0},{3,1},{4,6},{5,7},{6,4},{7,5},{8,10},{9,11},{10,... | collective-permute-start | bytes 1572872 | tf_op jit(solution)/shard_map/ppermute | solution.py:25
  110.0 6.5 %collective-permute-start.8 = (bf16[4,16,2048]{2,1,0:T(8,128)(2,1)S(1)}, bf16[4,16,2048]{2,1,0:T(8,128)(2,1)S(1)}, u32[]{:S(2)}, u32[]{:S(2)}) collective-permute-start(bf16[4,16,2048]{2,1,0:T(8,128)(2,1)S(1)} %fusion.51), channel_id=1, source_target_pairs={{0,2},{1,3},{2,0},{3,1},{4,6},{5,7},{6,4},{7,5},{8,10},{9,11},{10,... | collective-permute-start | bytes 786440 | tf_op jit(solution)/shard_map/ppermute | solution.py:25
  115.1 6.4 %collective-permute-start.10 = (bf16[4,16,2048]{2,1,0:T(8,128)(2,1)S(1)}, bf16[4,16,2048]{2,1,0:T(8,128)(2,1)S(1)}, u32[]{:S(2)}, u32[]{:S(2)}) collective-permute-start(bf16[4,16,2048]{2,1,0:T(8,128)(2,1)S(1)} %fusion.52), channel_id=1, source_target_pairs={{0,1},{1,0},{2,3},{3,2},{4,5},{5,4},{6,7},{7,6},{8,9},{9,8},{10,11... | collective-permute-start | bytes 786440 | tf_op jit(solution)/shard_map/ppermute | solution.py:25
  121.7 6.9 %collective-permute-start.11 = (bf16[1,16,4096]{2,1,0:T(8,128)(2,1)S(1)}, bf16[1,16,4096]{2,1,0:T(8,128)(2,1)S(1)}, u32[]{:S(2)}, u32[]{:S(2)}) collective-permute-start(bf16[1,16,4096]{2,1,0:T(8,128)(2,1)S(1)} %get-tuple-element.36), channel_id=1, source_target_pairs={{0,4},{1,5},{2,6},{3,7},{4,0},{5,1},{6,2},{7,3},{8,12},{9,13},{10,... | collective-permute-start | bytes 393224 | tf_op jit(solution)/shard_map/ppermute | solution.py:25
  121.9 12.9 %collective-permute-start.12 = (bf16[1,16,4096]{2,1,0:T(8,128)(2,1)S(1)}, bf16[1,16,4096]{2,1,0:T(8,128)(2,1)S(1)}, u32[]{:S(2)}, u32[]{:S(2)}) collective-permute-start(bf16[1,16,4096]{2,1,0:T(8,128)(2,1)S(1)} %get-tuple-element.38), channel_id=1, source_target_pairs={{0,8},{1,9},{2,10},{3,11},{4,12},{5,13},{6,14},{7,15},{8,0},{9,1},... | collective-permute-start | bytes 393224 | tf_op jit(solution)/shard_map/ppermute | solution.py:25
  123.0 11.8 %collective-permute-start.13 = (bf16[1,16,4096]{2,1,0:T(8,128)(2,1)S(1)}, bf16[1,16,4096]{2,1,0:T(8,128)(2,1)S(1)}, u32[]{:S(2)}, u32[]{:S(2)}) collective-permute-start(bf16[1,16,4096]{2,1,0:T(8,128)(2,1)S(1)} %get-tuple-element.37), channel_id=1, source_target_pairs={{0,12},{1,13},{2,14},{3,15},{4,8},{5,9},{6,10},{7,11},{8,4},{9,5},... | collective-permute-start | bytes 393224 | tf_op jit(solution)/shard_map/ppermute | solution.py:25
  135.2 5.4 %collective-permute-start.14 = (bf16[1,16,4096]{2,1,0:T(8,128)(2,1)S(1)}, bf16[1,16,4096]{2,1,0:T(8,128)(2,1)S(1)}, u32[]{:S(2)}, u32[]{:S(2)}) collective-permute-start(bf16[1,16,4096]{2,1,0:T(8,128)(2,1)S(1)} %fusion.69), channel_id=1, source_target_pairs={{0,4},{1,5},{2,6},{3,7},{4,0},{5,1},{6,2},{7,3},{8,12},{9,13},{10,... | collective-permute-start | bytes 393224 | tf_op jit(solution)/shard_map/ppermute | solution.py:25
  137.7 8.7 %collective-permute-start.15 = (bf16[1,16,4096]{2,1,0:T(8,128)(2,1)S(1)}, bf16[1,16,4096]{2,1,0:T(8,128)(2,1)S(1)}, u32[]{:S(2)}, u32[]{:S(2)}) collective-permute-start(bf16[1,16,4096]{2,1,0:T(8,128)(2,1)S(1)} %fusion.69), channel_id=1, source_target_pairs={{0,8},{1,9},{2,10},{3,11},{4,12},{5,13},{6,14},{7,15},{8,0},{9,1},... | collective-permute-start | bytes 393224 | tf_op jit(solution)/shard_map/ppermute | solution.py:25
  137.9 8.4 %collective-permute-start.16 = (bf16[1,16,4096]{2,1,0:T(8,128)(2,1)S(1)}, bf16[1,16,4096]{2,1,0:T(8,128)(2,1)S(1)}, u32[]{:S(2)}, u32[]{:S(2)}) collective-permute-start(bf16[1,16,4096]{2,1,0:T(8,128)(2,1)S(1)} %fusion.69), channel_id=1, source_target_pairs={{0,12},{1,13},{2,14},{3,15},{4,8},{5,9},{6,10},{7,11},{8,4},{9,5},... | collective-permute-start | bytes 393224 | tf_op jit(solution)/shard_map/ppermute | solution.py:25
  146.5 6.4 %collective-permute-start.19 = (bf16[4,16,2048]{2,1,0:T(8,128)(2,1)S(1)}, bf16[4,16,2048]{2,1,0:T(8,128)(2,1)S(1)}, u32[]{:S(2)}, u32[]{:S(2)}) collective-permute-start(bf16[4,16,2048]{2,1,0:T(8,128)(2,1)S(1)} %get-tuple-element.32), channel_id=1, source_target_pairs={{0,1},{1,0},{2,3},{3,2},{4,5},{5,4},{6,7},{7,6},{8,9},{9,8},{10,11... | collective-permute-start | bytes 786440 | tf_op jit(solution)/shard_map/ppermute | solution.py:25
  147.4 6.4 %collective-permute-start.17 = (bf16[4,16,2048]{2,1,0:T(8,128)(2,1)S(1)}, bf16[4,16,2048]{2,1,0:T(8,128)(2,1)S(1)}, u32[]{:S(2)}, u32[]{:S(2)}) collective-permute-start(bf16[4,16,2048]{2,1,0:T(8,128)(2,1)S(1)} %get-tuple-element.33), channel_id=1, source_target_pairs={{0,2},{1,3},{2,0},{3,1},{4,6},{5,7},{6,4},{7,5},{8,10},{9,11},{10,... | collective-permute-start | bytes 786440 | tf_op jit(solution)/shard_map/ppermute | solution.py:25
  153.1 9.2 %collective-permute-start.20 = (bf16[4,2,16,2048]{3,2,0,1:T(8,128)(2,1)S(1)}, bf16[4,2,16,2048]{3,2,0,1:T(8,128)(2,1)S(1)}, u32[]{:S(2)}, u32[]{:S(2)}) collective-permute-start(bf16[4,2,16,2048]{3,2,0,1:T(8,128)(2,1)S(1)} %get-tuple-element.35), channel_id=1, source_target_pairs={{0,2},{1,3},{2,0},{3,1},{4,6},{5,7},{6,4},{7,5},{8,10},{9,11},{10,... | collective-permute-start | bytes 1572872 | tf_op jit(solution)/shard_map/ppermute | solution.py:25
  154.7 9.7 %collective-permute-start.18 = (bf16[4,2,16,2048]{3,2,0,1:T(8,128)(2,1)S(1)}, bf16[4,2,16,2048]{3,2,0,1:T(8,128)(2,1)S(1)}, u32[]{:S(2)}, u32[]{:S(2)}) collective-permute-start(bf16[4,2,16,2048]{3,2,0,1:T(8,128)(2,1)S(1)} %get-tuple-element.29), channel_id=1, source_target_pairs={{0,1},{1,0},{2,3},{3,2},{4,5},{5,4},{6,7},{7,6},{8,9},{9,8},{10,11... | collective-permute-start | bytes 1572872 | tf_op jit(solution)/shard_map/ppermute | solution.py:25
  180.3 9.2 %collective-permute-start.21 = (bf16[4,2,16,2048]{3,2,0,1:T(8,128)(2,1)S(1)}, bf16[4,2,16,2048]{3,2,0,1:T(8,128)(2,1)S(1)}, u32[]{:S(2)}, u32[]{:S(2)}) collective-permute-start(bf16[4,2,16,2048]{3,2,0,1:T(8,128)(2,1)S(1)} %slice_bitcast_fusion.6), channel_id=1, source_target_pairs={{0,1},{1,0},{2,3},{3,2},{4,5},{5,4},{6,7},{7,6},{8,9},{9,8},{10,11... | collective-permute-start | bytes 1572872 | tf_op jit(solution)/shard_map/ppermute | solution.py:25
  182.4 9.4 %collective-permute-start.23 = (bf16[4,2,16,2048]{3,2,0,1:T(8,128)(2,1)S(1)}, bf16[4,2,16,2048]{3,2,0,1:T(8,128)(2,1)S(1)}, u32[]{:S(2)}, u32[]{:S(2)}) collective-permute-start(bf16[4,2,16,2048]{3,2,0,1:T(8,128)(2,1)S(1)} %slice_bitcast_fusion.4), channel_id=1, source_target_pairs={{0,2},{1,3},{2,0},{3,1},{4,6},{5,7},{6,4},{7,5},{8,10},{9,11},{10,... | collective-permute-start | bytes 1572872 | tf_op jit(solution)/shard_map/ppermute | solution.py:25
  190.9 6.4 %collective-permute-start.22 = (bf16[4,16,2048]{2,1,0:T(8,128)(2,1)S(1)}, bf16[4,16,2048]{2,1,0:T(8,128)(2,1)S(1)}, u32[]{:S(2)}, u32[]{:S(2)}) collective-permute-start(bf16[4,16,2048]{2,1,0:T(8,128)(2,1)S(1)} %fusion.53), channel_id=1, source_target_pairs={{0,2},{1,3},{2,0},{3,1},{4,6},{5,7},{6,4},{7,5},{8,10},{9,11},{10,... | collective-permute-start | bytes 786440 | tf_op jit(solution)/shard_map/ppermute | solution.py:25
  193.2 6.4 %collective-permute-start.24 = (bf16[4,16,2048]{2,1,0:T(8,128)(2,1)S(1)}, bf16[4,16,2048]{2,1,0:T(8,128)(2,1)S(1)}, u32[]{:S(2)}, u32[]{:S(2)}) collective-permute-start(bf16[4,16,2048]{2,1,0:T(8,128)(2,1)S(1)} %fusion.54), channel_id=1, source_target_pairs={{0,1},{1,0},{2,3},{3,2},{4,5},{5,4},{6,7},{7,6},{8,9},{9,8},{10,11... | collective-permute-start | bytes 786440 | tf_op jit(solution)/shard_map/ppermute | solution.py:25
  199.8 5.2 %collective-permute-start.25 = (bf16[1,16,4096]{2,1,0:T(8,128)(2,1)S(1)}, bf16[1,16,4096]{2,1,0:T(8,128)(2,1)S(1)}, u32[]{:S(2)}, u32[]{:S(2)}) collective-permute-start(bf16[1,16,4096]{2,1,0:T(8,128)(2,1)S(1)} %get-tuple-element.25), channel_id=1, source_target_pairs={{0,4},{1,5},{2,6},{3,7},{4,0},{5,1},{6,2},{7,3},{8,12},{9,13},{10,... | collective-permute-start | bytes 393224 | tf_op jit(solution)/shard_map/ppermute | solution.py:25
  202.0 8.7 %collective-permute-start.26 = (bf16[1,16,4096]{2,1,0:T(8,128)(2,1)S(1)}, bf16[1,16,4096]{2,1,0:T(8,128)(2,1)S(1)}, u32[]{:S(2)}, u32[]{:S(2)}) collective-permute-start(bf16[1,16,4096]{2,1,0:T(8,128)(2,1)S(1)} %get-tuple-element.27), channel_id=1, source_target_pairs={{0,8},{1,9},{2,10},{3,11},{4,12},{5,13},{6,14},{7,15},{8,0},{9,1},... | collective-permute-start | bytes 393224 | tf_op jit(solution)/shard_map/ppermute | solution.py:25
  202.3 8.4 %collective-permute-start.27 = (bf16[1,16,4096]{2,1,0:T(8,128)(2,1)S(1)}, bf16[1,16,4096]{2,1,0:T(8,128)(2,1)S(1)}, u32[]{:S(2)}, u32[]{:S(2)}) collective-permute-start(bf16[1,16,4096]{2,1,0:T(8,128)(2,1)S(1)} %get-tuple-element.26), channel_id=1, source_target_pairs={{0,12},{1,13},{2,14},{3,15},{4,8},{5,9},{6,10},{7,11},{8,4},{9,5},... | collective-permute-start | bytes 393224 | tf_op jit(solution)/shard_map/ppermute | solution.py:25
  214.6 8.0 %collective-permute-start.30 = (bf16[1,16,2048]{2,1,0:T(8,128)(2,1)S(1)}, bf16[1,16,2048]{2,1,0:T(8,128)(2,1)S(1)}, u32[]{:S(2)}, u32[]{:S(2)}) collective-permute-start(bf16[1,16,2048]{2,1,0:T(8,128)(2,1)S(1)} %fusion.77), channel_id=1, source_target_pairs={{0,8},{1,9},{2,10},{3,11},{4,12},{5,13},{6,14},{7,15},{8,0},{9,1},... | collective-permute-start | bytes 196616 | tf_op jit(solution)/shard_map/ppermute | solution.py:25
  214.9 7.8 %collective-permute-start.31 = (bf16[1,16,2048]{2,1,0:T(8,128)(2,1)S(1)}, bf16[1,16,2048]{2,1,0:T(8,128)(2,1)S(1)}, u32[]{:S(2)}, u32[]{:S(2)}) collective-permute-start(bf16[1,16,2048]{2,1,0:T(8,128)(2,1)S(1)} %fusion.77), channel_id=1, source_target_pairs={{0,12},{1,13},{2,14},{3,15},{4,8},{5,9},{6,10},{7,11},{8,4},{9,5},... | collective-permute-start | bytes 196616 | tf_op jit(solution)/shard_map/ppermute | solution.py:25
  227.1 5.0 %collective-permute-start.35 = (bf16[2,2,16,1024]{3,2,0,1:T(8,128)(2,1)S(1)}, bf16[2,2,16,1024]{3,2,0,1:T(8,128)(2,1)S(1)}, u32[]{:S(2)}, u32[]{:S(2)}) collective-permute-start(bf16[2,2,16,1024]{3,2,0,1:T(8,128)(2,1)S(1)} %get-tuple-element.66), channel_id=1, source_target_pairs={{0,2},{1,3},{2,0},{3,1},{4,6},{5,7},{6,4},{7,5},{8,10},{9,11},{10,... | collective-permute-start | bytes 393224 | tf_op jit(solution)/shard_map/ppermute | solution.py:25
  (29 other events, 286.6 us)
